TPU v7x, 32 devices: a whole 2x2x4 slice. The times are simulated.
32 devices in a mesh: rep: 4 (over x, core), shard: 8 (over z, y).
Axes of the slice: x: 2, y: 2, z: 4, core: 2. Of those that a mesh axis runs over, the one named last changes fastest.
Arguments:
- tokens: bfloat16 [16384, 768], P(('rep', 'shard')), may hold values from -6 to 6
- segment_ids: int32 [16384], P(('rep', 'shard')), may hold values from 0 to 511, never falling along the last dimension, each value on 1 to 512 neighbouring positions
- buckets: int32 [1023], replicated, may hold values from 0 to 31
- w_query: bfloat16 [768, 768], P('shard'), may hold values from -0.21875 to 0.21875
- w_key: bfloat16 [768, 768], P('shard'), may hold values from -0.21875 to 0.21875
- w_value: bfloat16 [768, 768], P('shard'), may hold values from -0.21875 to 0.21875
- w_output: bfloat16 [768, 768], P('shard'), may hold values from -0.625 to 0.625
- w_gate: bfloat16 [768, 2048], P('shard'), may hold values from -0.21875 to 0.21875
- w_up: bfloat16 [768, 2048], P('shard'), may hold values from -0.21875 to 0.21875
- w_down: bfloat16 [2048, 768], P('shard'), may hold values from -0.125 to 0.125
- norm_attn: bfloat16 [768], P('shard'), may hold values from 0.099609375 to 1.8984375
- norm_ffn: bfloat16 [768], P('shard'), may hold values from 0.099609375 to 1.8984375
- rel_bias: bfloat16 [32, 12], P('shard'), may hold values from -4 to 4
- cotangent: bfloat16 [16384, 768], P(('rep', 'shard')), may hold values from -6 to 6
Outputs:
- output: bfloat16 [16384, 768], P(('rep', 'shard'))
- grad_tokens: bfloat16 [16384, 768], P(('rep', 'shard'))
- grad_w_query: float32 [768, 768], P('shard')
- grad_w_key: float32 [768, 768], P('shard')
- grad_w_value: float32 [768, 768], P('shard')
- grad_w_output: float32 [768, 768], P('shard')
- grad_w_gate: float32 [768, 2048], P('shard')
- grad_w_up: float32 [768, 2048], P('shard')
- grad_w_down: float32 [2048, 768], P('shard')
- grad_norm_attn: float32 [768], P('shard')
- grad_norm_ffn: float32 [768], P('shard')
- grad_rel_bias: float32 [32, 12], P('shard')
Inputs may be any that keep to these rules, and one draw needn't show every extreme that they name: `segment_ids`: ids never fall along the bytes; a document holds 1 to 512 bytes. `buckets`: entry j - i + 511 is the bucket of key j seen from query i of one sequence.
All inputs are finite; a program needn't handle non-finite values.
Results may differ from a plain program's by a relative error of at most 0.019.
Values may be sent and summed in bfloat16 or wider, within the bound.
No kernel may reach another device: no remote copies, remote signals or barrier semaphores. Data moves between devices by JAX's collectives and lax.ppermute only.
A program may use at most 192 MiB of HBM per device.

v0:
```python
import jax
import jax.numpy as jnp
from jax import lax
from jax.sharding import PartitionSpec as P

D = 768
HEADS = 12
HD = 64
NB = 32
EPSILON = 1e-06
HIGHEST = lax.Precision.HIGHEST


def product(left_op, right_op):
    return jnp.dot(left_op, right_op, preferred_element_type=jnp.float32)


def product_tn(left_op, right_op):
    return lax.dot_general(
        left_op, right_op, (((0,), (0,)), ((), ())), preferred_element_type=jnp.float32
    )


def product_nt(left_op, right_op):
    return lax.dot_general(
        left_op, right_op, (((1,), (1,)), ((), ())), preferred_element_type=jnp.float32
    )


def gelu_tanh(values):
    return jax.nn.gelu(values, approximate=True)


def normalize(values, gain_vec):
    inverse = lax.rsqrt(jnp.mean(values * values, axis=-1, keepdims=True) + EPSILON)
    return (values * inverse * gain_vec, inverse)


def normalize_back(grad_out, values, inverse, gain_vec):
    unit_rows = values * inverse
    grad_gain = jnp.sum(grad_out * unit_rows, axis=0)
    scaled = grad_out * gain_vec
    grad_in = inverse * (scaled - unit_rows * jnp.mean(scaled * unit_rows, axis=-1, keepdims=True))
    return (grad_in, grad_gain)


def toeplitz_rows(table_low, block_start, block_rows, length):
    heads = table_low.shape[0]
    padded = jnp.pad(table_low, ((0, 0), (0, 1)))
    tiled = jnp.broadcast_to(padded[:, None, :], (heads, block_rows, 2 * length))
    flat = tiled.reshape(heads, block_rows * 2 * length)[:, : block_rows * (2 * length - 1)]
    skewed = flat.reshape(heads, block_rows, 2 * length - 1)
    return lax.dynamic_slice_in_dim(skewed, length - 1 - block_start, length, 2)


def diagonal_sums(grad_low, block_start, length):
    heads, block_rows, unused_keys = grad_low.shape
    width = 2 * length - 1 + block_rows
    zero_index = jnp.zeros((), jnp.int32)
    placed = lax.dynamic_update_slice(
        jnp.zeros((heads, block_rows, width), jnp.bfloat16),
        grad_low,
        (zero_index, zero_index, length - 1 - block_start),
    )
    flat = jnp.pad(placed.reshape(heads, block_rows * width), ((0, 0), (0, block_rows)))
    sheared = flat.reshape(heads, block_rows, width + 1)[:, :, : 2 * length - 1]
    return jnp.sum(sheared, axis=1, dtype=jnp.float32)


def block_scores(query_block, segment_block, block_start, key_rows, segment_ids, table_low):
    block_rows = query_block.shape[0]
    length = key_rows.shape[0]
    raw_scores = jnp.einsum(
        "qhd,khd->hqk", query_block, key_rows, preferred_element_type=jnp.float32
    ) * HD ** (-0.5)
    rel_terms = toeplitz_rows(table_low, block_start, block_rows, length)
    same_doc = segment_block[:, None] == segment_ids[None, :]
    return jnp.where(same_doc[None], raw_scores + rel_terms.astype(jnp.float32), -1000000000.0)


def block_inputs(queries, segment_ids):
    length = queries.shape[0]
    block_rows = min(512, length)
    block_count = length // block_rows
    return (
        queries.reshape(block_count, block_rows, HEADS, HD),
        segment_ids.reshape(block_count, block_rows),
        jnp.arange(block_count, dtype=jnp.int32) * block_rows,
    )


def forward(weights, tokens_f, segment_ids, buckets):
    (
        query_full,
        key_full,
        value_full,
        output_full,
        gate_full,
        up_full,
        down_full,
        attn_gain,
        ffn_gain,
        bias_full,
    ) = weights
    length = tokens_f.shape[0]
    normed_one, inverse_one = normalize(tokens_f, attn_gain.astype(jnp.float32))
    normed_one = normed_one.astype(jnp.bfloat16)
    queries = product(normed_one, query_full).astype(jnp.bfloat16).reshape(length, HEADS, HD)
    key_rows = product(normed_one, key_full).astype(jnp.bfloat16).reshape(length, HEADS, HD)
    value_rows = product(normed_one, value_full).astype(jnp.bfloat16).reshape(length, HEADS, HD)
    bucket_onehot = (buckets[:, None] == jnp.arange(NB, dtype=jnp.int32)[None, :]).astype(
        jnp.bfloat16
    )
    table_low = product(bucket_onehot, bias_full).T.astype(jnp.bfloat16)

    def attend(inputs):
        query_block, segment_block, block_start = inputs
        scores = block_scores(
            query_block, segment_block, block_start, key_rows, segment_ids, table_low
        )
        row_peak = jnp.max(scores, axis=-1, keepdims=True)
        weights_exp = jnp.exp(scores - row_peak)
        row_total = jnp.sum(weights_exp, axis=-1, keepdims=True)
        prob_rows = (weights_exp / row_total).astype(jnp.bfloat16)
        block_out = jnp.einsum(
            "hqk,khd->qhd", prob_rows, value_rows, preferred_element_type=jnp.float32
        )
        return (block_out.astype(jnp.bfloat16), row_peak + jnp.log(row_total))

    attended, log_total = lax.map(attend, block_inputs(queries, segment_ids))
    attended = attended.reshape(length, D)
    middle = tokens_f + product(attended, output_full)
    normed_two, inverse_two = normalize(middle, ffn_gain.astype(jnp.float32))
    normed_two = normed_two.astype(jnp.bfloat16)
    gate_pre = product(normed_two, gate_full)
    up_part = product(normed_two, up_full)
    hidden = (gelu_tanh(gate_pre) * up_part).astype(jnp.bfloat16)
    output = middle + product(hidden, down_full)
    kept_acts = (
        normed_one,
        inverse_one,
        queries,
        key_rows,
        value_rows,
        table_low,
        attended,
        log_total,
        middle,
        normed_two,
        inverse_two,
        gate_pre,
        up_part,
        hidden,
    )
    return (output, kept_acts)


def shards(
    tokens,
    segment_ids,
    buckets,
    w_query,
    w_key,
    w_value,
    w_output,
    w_gate,
    w_up,
    w_down,
    norm_attn,
    norm_ffn,
    rel_bias,
    cotangent,
):
    gathered = (
        lax.all_gather(w_query, "shard", axis=0, tiled=True),
        lax.all_gather(w_key, "shard", axis=0, tiled=True),
        lax.all_gather(w_value, "shard", axis=0, tiled=True),
        lax.all_gather(w_output, "shard", axis=0, tiled=True),
        lax.all_gather(w_gate, "shard", axis=0, tiled=True),
        lax.all_gather(w_up, "shard", axis=0, tiled=True),
        lax.all_gather(w_down, "shard", axis=0, tiled=True),
        lax.all_gather(norm_attn, "shard", axis=0, tiled=True),
        lax.all_gather(norm_ffn, "shard", axis=0, tiled=True),
        lax.all_gather(rel_bias, "shard", axis=0, tiled=True),
    )
    tokens_f = tokens.astype(jnp.float32)
    length = tokens_f.shape[0]
    output, kept_acts = forward(gathered, tokens_f, segment_ids, buckets)
    back_weights = (
        lax.all_gather(w_query, "shard", axis=0, tiled=True),
        lax.all_gather(w_key, "shard", axis=0, tiled=True),
        lax.all_gather(w_value, "shard", axis=0, tiled=True),
        lax.all_gather(w_output, "shard", axis=0, tiled=True),
        lax.all_gather(w_gate, "shard", axis=0, tiled=True),
        lax.all_gather(w_up, "shard", axis=0, tiled=True),
        lax.all_gather(w_down, "shard", axis=0, tiled=True),
        lax.all_gather(norm_attn, "shard", axis=0, tiled=True),
        lax.all_gather(norm_ffn, "shard", axis=0, tiled=True),
        lax.all_gather(rel_bias, "shard", axis=0, tiled=True),
    )
    unused_out, kept_acts = forward(back_weights, tokens_f, segment_ids, buckets)
    (
        query_full,
        key_full,
        value_full,
        output_full,
        gate_full,
        up_full,
        down_full,
        attn_gain,
        ffn_gain,
        bias_full,
    ) = back_weights
    (
        normed_one,
        inverse_one,
        queries,
        key_rows,
        value_rows,
        table_low,
        attended,
        log_total,
        middle,
        normed_two,
        inverse_two,
        gate_pre,
        up_part,
        hidden,
    ) = kept_acts
    grad_out = cotangent.astype(jnp.float32)
    grad_w_down = product_tn(hidden, cotangent)
    grad_hidden = product_nt(cotangent, down_full)
    activated, gelu_pull = jax.vjp(gelu_tanh, gate_pre)
    grad_gate = gelu_pull(grad_hidden * up_part)[0].astype(jnp.bfloat16)
    grad_up = (grad_hidden * activated).astype(jnp.bfloat16)
    grad_w_gate = product_tn(normed_two, grad_gate)
    grad_w_up = product_tn(normed_two, grad_up)
    grad_normed_two = product_nt(grad_gate, gate_full) + product_nt(grad_up, up_full)
    grad_middle_part, grad_norm_ffn = normalize_back(
        grad_normed_two, middle, inverse_two, ffn_gain.astype(jnp.float32)
    )
    grad_middle = grad_out + grad_middle_part
    grad_branch = grad_middle.astype(jnp.bfloat16)
    grad_w_output = product_tn(attended, grad_branch)
    grad_attended = (
        product_nt(grad_branch, output_full).astype(jnp.bfloat16).reshape(length, HEADS, HD)
    )
    query_blocks, segment_blocks, block_starts = block_inputs(queries, segment_ids)
    grad_att_blocks = grad_attended.reshape(query_blocks.shape)

    def attend_back(carry_acc, inputs):
        grad_keys, grad_values, grad_offsets = carry_acc
        query_block, segment_block, block_start, grad_block, log_block = inputs
        scores = block_scores(
            query_block, segment_block, block_start, key_rows, segment_ids, table_low
        )
        prob_rows = jnp.exp(scores - log_block)
        grad_probs = jnp.einsum(
            "qhd,khd->hqk", grad_block, value_rows, preferred_element_type=jnp.float32
        )
        grad_scores = prob_rows * (
            grad_probs - jnp.sum(prob_rows * grad_probs, axis=-1, keepdims=True)
        )
        grad_low = grad_scores.astype(jnp.bfloat16)
        grad_query = jnp.einsum(
            "hqk,khd->qhd", grad_low, key_rows, preferred_element_type=jnp.float32
        ) * HD ** (-0.5)
        grad_keys = grad_keys + jnp.einsum(
            "hqk,qhd->khd", grad_low, query_block, preferred_element_type=jnp.float32
        ) * HD ** (-0.5)
        grad_values = grad_values + jnp.einsum(
            "hqk,qhd->khd",
            prob_rows.astype(jnp.bfloat16),
            grad_block,
            preferred_element_type=jnp.float32,
        )
        diagonal = diagonal_sums(grad_low, block_start, length)
        return ((grad_keys, grad_values, grad_offsets + diagonal), grad_query)

    zero_rows = jnp.zeros((length, HEADS, HD), jnp.float32)
    zero_offsets = jnp.zeros((HEADS, 2 * length - 1), jnp.float32)
    (grad_keys, grad_values, grad_offsets), grad_q_blocks = lax.scan(
        attend_back,
        (zero_rows, zero_rows, zero_offsets),
        (query_blocks, segment_blocks, block_starts, grad_att_blocks, log_total),
    )
    grad_queries = grad_q_blocks.reshape(length, D).astype(jnp.bfloat16)
    grad_key_rows = grad_keys.reshape(length, D).astype(jnp.bfloat16)
    grad_value_rows = grad_values.reshape(length, D).astype(jnp.bfloat16)
    grad_w_query = product_tn(normed_one, grad_queries)
    grad_w_key = product_tn(normed_one, grad_key_rows)
    grad_w_value = product_tn(normed_one, grad_value_rows)
    grad_normed_one = (
        product_nt(grad_queries, query_full)
        + product_nt(grad_key_rows, key_full)
        + product_nt(grad_value_rows, value_full)
    )
    grad_tokens_part, grad_norm_attn = normalize_back(
        grad_normed_one, tokens_f, inverse_one, attn_gain.astype(jnp.float32)
    )
    grad_tokens = (grad_middle + grad_tokens_part).astype(jnp.bfloat16)
    bucket_onehot = (buckets[:, None] == jnp.arange(NB, dtype=jnp.int32)[None, :]).astype(
        jnp.float32
    )
    grad_rel_bias = jnp.dot(
        bucket_onehot.T, grad_offsets.T, precision=HIGHEST, preferred_element_type=jnp.float32
    )
    (
        share_query,
        share_key,
        share_value,
        share_output,
        share_gate,
        share_up,
        share_down,
        share_attn,
        share_ffn,
        share_bias,
    ) = (
        lax.psum_scatter(
            grad_w_query.astype(jnp.bfloat16), "shard", scatter_dimension=0, tiled=True
        ).astype(jnp.float32),
        lax.psum_scatter(
            grad_w_key.astype(jnp.bfloat16), "shard", scatter_dimension=0, tiled=True
        ).astype(jnp.float32),
        lax.psum_scatter(
            grad_w_value.astype(jnp.bfloat16), "shard", scatter_dimension=0, tiled=True
        ).astype(jnp.float32),
        lax.psum_scatter(
            grad_w_output.astype(jnp.bfloat16), "shard", scatter_dimension=0, tiled=True
        ).astype(jnp.float32),
        lax.psum_scatter(
            grad_w_gate.astype(jnp.bfloat16), "shard", scatter_dimension=0, tiled=True
        ).astype(jnp.float32),
        lax.psum_scatter(
            grad_w_up.astype(jnp.bfloat16), "shard", scatter_dimension=0, tiled=True
        ).astype(jnp.float32),
        lax.psum_scatter(
            grad_w_down.astype(jnp.bfloat16), "shard", scatter_dimension=0, tiled=True
        ).astype(jnp.float32),
        lax.psum_scatter(
            grad_norm_attn.astype(jnp.bfloat16), "shard", scatter_dimension=0, tiled=True
        ).astype(jnp.float32),
        lax.psum_scatter(
            grad_norm_ffn.astype(jnp.bfloat16), "shard", scatter_dimension=0, tiled=True
        ).astype(jnp.float32),
        lax.psum_scatter(
            grad_rel_bias.astype(jnp.bfloat16), "shard", scatter_dimension=0, tiled=True
        ).astype(jnp.float32),
    )
    totals = (
        lax.psum(share_query.astype(jnp.bfloat16), "rep").astype(jnp.float32),
        lax.psum(share_key.astype(jnp.bfloat16), "rep").astype(jnp.float32),
        lax.psum(share_value.astype(jnp.bfloat16), "rep").astype(jnp.float32),
        lax.psum(share_output.astype(jnp.bfloat16), "rep").astype(jnp.float32),
        lax.psum(share_gate.astype(jnp.bfloat16), "rep").astype(jnp.float32),
        lax.psum(share_up.astype(jnp.bfloat16), "rep").astype(jnp.float32),
        lax.psum(share_down.astype(jnp.bfloat16), "rep").astype(jnp.float32),
        lax.psum(share_attn.astype(jnp.bfloat16), "rep").astype(jnp.float32),
        lax.psum(share_ffn.astype(jnp.bfloat16), "rep").astype(jnp.float32),
        lax.psum(share_bias.astype(jnp.bfloat16), "rep").astype(jnp.float32),
    )
    return (
        output.astype(jnp.bfloat16),
        grad_tokens,
        totals[0],
        totals[1],
        totals[2],
        totals[3],
        totals[4],
        totals[5],
        totals[6],
        totals[7],
        totals[8],
        totals[9],
    )


def solution(mesh):
    return jax.shard_map(
        shards,
        mesh=mesh,
        in_specs=(
            P(("rep", "shard"), None),
            P(("rep", "shard")),
            P(),
            P("shard", None),
            P("shard", None),
            P("shard", None),
            P("shard", None),
            P("shard", None),
            P("shard", None),
            P("shard", None),
            P("shard"),
            P("shard"),
            P("shard", None),
            P(("rep", "shard"), None),
        ),
        out_specs=(
            P(("rep", "shard"), None),
            P(("rep", "shard"), None),
            P("shard", None),
            P("shard", None),
            P("shard", None),
            P("shard", None),
            P("shard", None),
            P("shard", None),
            P("shard", None),
            P("shard"),
            P("shard"),
            P("shard", None),
        ),
        check_vma=False,
    )
```

profile of v0, /device:TPU:0, one launch (start us, length us, event | category | flops | bytes accessed | tf_op | source)
XLA Modules:
  0.0 968.3 jit_solution(6518679605670658426)
XLA Ops:
  15.6 23.2 %all-reduce.9 = (bf16[768]{0:T(1024)(128)(2,1)S(1)}, bf16[768]{0:T(1024)(128)(2,1)S(1)}) all-reduce(bf16[768]{0:T(1024)(128)(2,1)S(1)} %dynamic-update-slice, bf16[768]{0:T(1024)(128)(2,1)S(1)} %dynamic-update-slice.1), channel_id=1, replica_groups=mesh['rep'=4,'shard'=8] {'shard'}, use_global_device_ids=true, to_apply=%add.3 | all-reduce | flops 1536 | bytes 6144
  39.1 16.5 %all-gather = bf16[8,4,12]{2,1,0:T(4,128)(2,1)S(1)} all-gather(bf16[1,4,12]{2,1,0:T(4,128)(2,1)S(1)} %bitcast.97), channel_id=1, replica_groups=mesh['rep'=4,'shard'=8] {'shard'}, dimensions={0}, use_global_device_ids=true | all-gather | bytes 864 | tf_op jit(solution)/shard_map/all_gather | solution.py:184
  55.9 6.1 broadcast_in_dim.120
  62.0 5.8 pad.17
  67.8 29.2 %copy.64 = bf16[2,8,512,1024]{3,1,2,0:T(8,128)(2,1)S(1)} copy(bf16[2,8,512,1024]{3,2,1,0:T(8,128)(2,1)S(1)} %bitcast.78) | data formatting | bytes 33554432
  97.1 6.6 slice.15
  103.7 36.8 %reshape.147 = bf16[12,512,1023]{2,1,0:T(8,128)(2,1)} reshape(bf16[12,523776]{1,0:T(8,128)(2,1)} %slice.15) | data formatting | bytes 25141248 | tf_op jit(solution)/shard_map/while/body/eval_jaxpr/reshape | solution.py:52
  140.4 9.7 %dynamic_slice.35 = bf16[12,512,512]{2,1,0:T(8,128)(2,1)} slice(bf16[12,512,1023]{2,1,0:T(8,128)(2,1)} %reshape.147), slice={[0:12], [0:512], [511:1023]} | slice | bytes 12582912 | tf_op jit(solution)/shard_map/while/body/eval_jaxpr/dynamic_slice | solution.py:53
  150.2 8.7 copy.62
  159.1 2.1 convolution_convert_fusion.10
  161.3 2.1 convolution_convert_fusion.9
  164.0 3.3 convolution_convert_fusion.8
  168.7 5.3 fusion.43
  175.9 2.7 copy-done
  178.5 2.9 fusion.28
  181.5 2.5 multiply_reduce_fusion.3
  185.3 55.6 %all-gather.17.cloned.1.call-done = bf16[768,2048]{1,0:T(8,128)(2,1)} async-done(((bf16[96,2048]{1,0:T(8,128)(2,1)}), bf16[768,2048]{1,0:T(8,128)(2,1)}) %all-gather.17.cloned.1.call-update) | async-done | bytes 3145744 | tf_op jit(solution)/shard_map/all_gather | solution.py:179
  241.0 5.6 fusion.44
  246.6 55.1 %all-gather.19.cloned.1.call-done = bf16[768,2048]{1,0:T(8,128)(2,1)} async-done(((bf16[96,2048]{1,0:T(8,128)(2,1)}), bf16[768,2048]{1,0:T(8,128)(2,1)}) %all-gather.19.cloned.1.call-update) | async-done | bytes 3145744 | tf_op jit(solution)/shard_map/all_gather | solution.py:180
  301.7 5.6 fusion.45
  307.4 55.2 %all-gather.21.cloned.1.call-done = bf16[2048,768]{1,0:T(8,128)(2,1)} async-done(((bf16[256,768]{1,0:T(8,128)(2,1)}), bf16[2048,768]{1,0:T(8,128)(2,1)}) %all-gather.21.cloned.1.call-update) | async-done | bytes 3145744 | tf_op jit(solution)/shard_map/all_gather | solution.py:181
  362.6 8.7 multiply_convert_fusion.1
  375.2 2.1 multiply_reduce_fusion.1
  381.7 10.6 %multiply_reduce_fusion = (f32[12,512]{1,0:T(8,128)S(1)}, f32[12,512,512]{1,2,0:T(8,128)}) fusion(f32[12,512,512]{1,2,0:T(8,128)} %copy-done, f32[12,512]{1,0:T(8,128)S(1)} %log_add_fusion, bf16[512,12,64]{0,2,1:T(8,128)(2,1)S(1)} %bitcast.82, bf16[512,12,64]{0,2,1:T(8,128)(2,1)} %bitcast.87), kind=kOutput, calls=%fused_computation.2 | convolution fusion | flops 412084224 | bytes 26787840 | tf_op jit(solution)/shard_map/while/body/eval_jaxpr/qhd,khd->hqk/dot_general | solution.py:258
  394.6 7.0 multiply_convert_fusion
  407.1 5.1 multiply_convert_fusion.3
  415.2 6.6 fusion.25
  426.7 5.4 convolution_convert_fusion.2
  433.2 5.1 convolution_convert_fusion.1
  439.4 5.1 convolution_convert_fusion
  445.9 8.7 copy.63
  454.5 9.3 dynamic_update_slice.15.clone
  463.9 69.5 %reshape.149 = bf16[12,785920]{1,0:T(8,128)(2,1)} reshape(bf16[12,512,1535]{2,1,0:T(8,128)(2,1)} %dynamic_update_slice.15.clone) | data formatting | bytes 37724160 | tf_op jit(solution)/shard_map/while/body/eval_jaxpr/reshape | solution.py:65
  533.4 13.1 %pad.16 = bf16[12,786432]{1,0:T(8,128)(2,1)S(1)} pad(bf16[12,785920]{1,0:T(8,128)(2,1)} %reshape.149, bf16[]{:T(256)} %constant.111.clone.1), padding=0_0x0_512 | pad | bytes 37736448 | tf_op jit(solution)/shard_map/while/body/eval_jaxpr/jit(_pad)/pad | solution.py:65
  546.5 19.4 %copy.65 = bf16[2,8,512,1536]{3,2,1,0:T(8,128)(2,1)} copy(bf16[2,8,512,1536]{3,1,2,0:T(8,128)(2,1)S(1)} %bitcast.76) | data formatting | bytes 50331648
  565.9 16.7 %slice.17 = bf16[12,512,1536]{2,1,0:T(8,128)(2,1)} slice(bf16[16,512,1536]{2,1,0:T(8,128)(2,1)} %bitcast.77), slice={[0:12], [0:512], [0:1536]} | slice | bytes 37748736 | tf_op jit(solution)/shard_map/while/body/eval_jaxpr/reshape | solution.py:66
  582.5 7.8 convert_reduce_fusion
  590.9 2.2 fusion.47
  594.7 2.4 fusion.23
  597.0 34.9 %all-reduce.8 = (bf16[768]{0:T(1024)(128)(2,1)S(1)}, bf16[768]{0:T(1024)(128)(2,1)S(1)}, bf16[32,12]{1,0:T(8,128)(2,1)S(1)}) all-reduce(bf16[768]{0:T(1024)(128)(2,1)S(1)} %get-tuple-element.78, bf16[768]{0:T(1024)(128)(2,1)S(1)} %get-tuple-element.76, ...), channel_id=9, replica_groups=mesh['rep'=4,'shard'=8] {'shard'}, use_global_device_ids=true, to_apply=%region_22.23.clone | all-reduce | flops 1920 | bytes 7680
  632.1 6.0 all-reduce.10
  639.8 32.4 %reduce-scatter.14.cloned.1.call-done = bf16[96,768]{1,0:T(8,128)(2,1)} async-done(((bf16[768,768]{1,0:T(8,128)(2,1)}), bf16[96,768]{1,0:T(8,128)(2,1)}) %reduce-scatter.14.cloned.1.call-update) | async-done | bytes 147472 | tf_op jit(solution)/shard_map/reduce_scatter | solution.py:329
  672.2 77.1 %reduce-scatter.16.cloned.1.call-done = bf16[96,2048]{1,0:T(8,128)(2,1)} async-done(((bf16[768,2048]{1,0:T(8,128)(2,1)}), bf16[96,2048]{1,0:T(8,128)(2,1)}) %reduce-scatter.16.cloned.1.call-update) | async-done | bytes 393232 | tf_op jit(solution)/shard_map/reduce_scatter | solution.py:332
  749.3 76.8 %reduce-scatter.18.cloned.1.call-done = bf16[96,2048]{1,0:T(8,128)(2,1)} async-done(((bf16[768,2048]{1,0:T(8,128)(2,1)}), bf16[96,2048]{1,0:T(8,128)(2,1)}) %reduce-scatter.18.cloned.1.call-update) | async-done | bytes 393232 | tf_op jit(solution)/shard_map/reduce_scatter | solution.py:335
  826.1 76.8 %reduce-scatter.20.cloned.1.call-done = bf16[256,768]{1,0:T(8,128)(2,1)} async-done(((bf16[2048,768]{1,0:T(8,128)(2,1)}), bf16[256,768]{1,0:T(8,128)(2,1)}) %reduce-scatter.20.cloned.1.call-update) | async-done | bytes 393232 | tf_op jit(solution)/shard_map/reduce_scatter | solution.py:338
  903.0 2.9 fusion.22
  905.9 4.3 add_convert_fusion
  910.2 40.8 %all-reduce.14.cloned.1.call-done = (bf16[96,768]{1,0:T(8,128)(2,1)}, bf16[96,768]{1,0:T(8,128)(2,1)}, bf16[96,768]{1,0:T(8,128)(2,1)}, bf16[96,768]{1,0:T(8,128...) async-done(((bf16[96,768]{1,0:T(8,128)(2,1)}, bf16[96,768]{1,0:T(8,128)(2,1)}, bf16[96,768]{1,0:T(8,128)(2,1)}, ...) | async-done | bytes 1769488 | tf_op jit(solution)/shard_map/psum | solution.py:352
  (160 shorter events, 54.2 us)
Async XLA Ops:
  7.2 31.6 %copy-start.2 = (bf16[512,768]{1,0:T(8,128)(2,1)S(1)}, bf16[512,768]{1,0:T(8,128)(2,1)}, u32[]{:S(2)}) copy-start(bf16[512,768]{1,0:T(8,128)(2,1)} %param.14) | copy-start | bytes 2359300
  7.2 31.9 %copy-start.26 = (bf16[4,12]{1,0:T(4,128)(2,1)S(1)}, bf16[4,12]{1,0:T(4,128)(2,1)}, u32[]{:S(2)}) copy-start(bf16[4,12]{1,0:T(4,128)(2,1)} %param.26) | copy-start | bytes 292
  7.2 48.3 %copy-start.32 = (s32[1023]{0:T(1024)S(1)}, s32[1023]{0:T(1024)}, u32[]{:S(2)}) copy-start(s32[1023]{0:T(1024)} %param.16) | copy-start | bytes 12280
  7.2 151.9 %all-gather.9.cloned.1.call-start = ((), (), s32[]{:S(2)}) async-start(), calls=%async_computation.7 | async-start | bytes 1327104 | tf_op jit(solution)/shard_map/all_gather | solution.py:177
  7.9 153.3 %all-gather.11.cloned.1.call-start = ((), (), s32[]{:S(2)}) async-start(), calls=%async_computation.8 | async-start | bytes 1327104 | tf_op jit(solution)/shard_map/all_gather | solution.py:175
  8.7 155.3 %all-gather.13.cloned.1.call-start = ((), (), s32[]{:S(2)}) async-start(), calls=%async_computation.9 | async-start | bytes 1327104 | tf_op jit(solution)/shard_map/all_gather | solution.py:176
  9.4 172.0 %all-gather.15.cloned.1.call-start = ((), (), s32[]{:S(2)}) async-start(), calls=%async_computation.10 | async-start | bytes 1327104 | tf_op jit(solution)/shard_map/all_gather | solution.py:178
  10.0 231.0 %all-gather.17.cloned.1.call-start = ((), (), s32[]{:S(2)}) async-start(), calls=%async_computation.11 | async-start | bytes 3538944 | tf_op jit(solution)/shard_map/all_gather | solution.py:179
  10.6 291.1 %all-gather.19.cloned.1.call-start = ((), (), s32[]{:S(2)}) async-start(), calls=%async_computation.12 | async-start | bytes 3538944 | tf_op jit(solution)/shard_map/all_gather | solution.py:180
  11.2 351.4 %all-gather.21.cloned.1.call-start = ((), (), s32[]{:S(2)}) async-start(), calls=%async_computation.13 | async-start | bytes 3538944 | tf_op jit(solution)/shard_map/all_gather | solution.py:181
  11.9 627.9 %reduce-scatter.8.cloned.1.call-start = ((), (), s32[]{:S(2)}) async-start(), calls=%async_computation.14 | async-start | bytes 1327104 | tf_op jit(solution)/shard_map/reduce_scatter | solution.py:320
  150.2 8.7 copy-start.25
  163.7 12.2 %copy-start.9 = (bf16[512,768]{0,1:T(8,128)(2,1)}, bf16[512,768]{0,1:T(8,128)(2,1)S(1)}, u32[]{:S(2)}) copy-start(bf16[512,768]{0,1:T(8,128)(2,1)S(1)} %copy.48) | copy-start | bytes 2359300
  164.0 4.7 copy-start.5
  174.0 4.5 copy-start
  181.4 2.5 copy-start.15
  183.9 1.2 copy-start.6
  185.3 116.4 %copy-start.17 = (bf16[512,768]{1,0:T(8,128)(2,1)}, bf16[512,768]{1,0:T(8,128)(2,1)S(1)}, u32[]{:S(2)}) copy-start(bf16[512,768]{1,0:T(8,128)(2,1)S(1)} %multiply_convert_fusion.5) | copy-start | bytes 2359300
  246.6 116.0 %copy-start.19 = (bf16[512,768]{1,0:T(8,128)(2,1)S(1)}, bf16[512,768]{1,0:T(8,128)(2,1)}, u32[]{:S(2)}) copy-start(bf16[512,768]{1,0:T(8,128)(2,1)} %param.27) | copy-start | bytes 2359300
  362.6 8.7 copy-start.28
  371.3 1.9 copy-start.35
  371.3 2.1 copy-start.34
  371.3 2.6 copy-start.7
  371.3 3.9 copy-start.29
  377.3 1.3 copy-start.31
  381.7 10.7 %slice-start = ((s8[12582912]{0:T(1024)(128)(4,1)}), s8[4194304]{0:T(1024)(128)(4,1)S(1)}, s32[]{:S(2)}) async-start(s8[12582912]{0:T(1024)(128)(4,1)} %bitcast.74), calls=%async_computation.22 | async-start | bytes 8388608
  381.7 11.6 %slice-start.1 = ((s8[12582912]{0:T(1024)(128)(4,1)}), s8[4194304]{0:T(1024)(128)(4,1)S(1)}, s32[]{:S(2)}) async-start(s8[12582912]{0:T(1024)(128)(4,1)} %bitcast.74), calls=%async_computation.23 | async-start | bytes 8388608
  381.7 12.8 %slice-start.2 = ((s8[12582912]{0:T(1024)(128)(4,1)}), s8[4194304]{0:T(1024)(128)(4,1)S(1)}, s32[]{:S(2)}) async-start(s8[12582912]{0:T(1024)(128)(4,1)} %bitcast.74), calls=%async_computation.24 | async-start | bytes 8388608
  401.5 2.6 copy-start.1
  401.6 3.5 copy-start.3
  407.0 6.0 copy-start.4
  407.0 232.8 %reduce-scatter.10.cloned.1.call-start = ((), (), s32[]{:S(2)}) async-start(), calls=%async_computation.15 | async-start | bytes 1327104 | tf_op jit(solution)/shard_map/reduce_scatter | solution.py:323
  415.1 224.7 %reduce-scatter.12.cloned.1.call-start = ((), (), s32[]{:S(2)}) async-start(), calls=%async_computation.16 | async-start | bytes 1327104 | tf_op jit(solution)/shard_map/reduce_scatter | solution.py:326
  422.7 2.1 copy-start.16
  424.7 247.5 %reduce-scatter.14.cloned.1.call-start = ((), (), s32[]{:S(2)}) async-start(), calls=%async_computation.17 | async-start | bytes 1327104 | tf_op jit(solution)/shard_map/reduce_scatter | solution.py:329
  426.6 322.7 %reduce-scatter.16.cloned.1.call-start = ((), (), s32[]{:S(2)}) async-start(), calls=%async_computation.18 | async-start | bytes 3538944 | tf_op jit(solution)/shard_map/reduce_scatter | solution.py:332
  432.1 394.0 %reduce-scatter.18.cloned.1.call-start = ((), (), s32[]{:S(2)}) async-start(), calls=%async_computation.19 | async-start | bytes 3538944 | tf_op jit(solution)/shard_map/reduce_scatter | solution.py:335
  438.3 464.6 %reduce-scatter.20.cloned.1.call-start = ((), (), s32[]{:S(2)}) async-start(), calls=%async_computation.20 | async-start | bytes 3538944 | tf_op jit(solution)/shard_map/reduce_scatter | solution.py:338
  444.5 506.5 %all-reduce.14.cloned.1.call-start = ((), (), s32[]{:S(2)}) async-start(), calls=%async_computation.21 | async-start | bytes 3538944 | tf_op jit(solution)/shard_map/psum | solution.py:352
  582.5 7.8 copy-start.33
  582.5 8.4 copy-start.13
  590.3 2.8 copy-start.22
  590.3 2.8 copy-start.30
  593.2 1.5 copy-start.14
  903.0 2.9 copy-start.8
  903.0 2.9 copy-start.27
  951.0 8.6 copy-start.24
  951.0 9.5 copy-start.23
  (6 other events, 6.1 us)
Sparse Core Ops, SparseCore 0:
  10.2 43.9 all-gather.8
  56.4 39.8 all-gather.10
  98.5 39.7 all-gather.12
  140.3 39.7 all-gather.14
  182.2 58.7 all-gather.16
  243.0 58.6 all-gather.18
  303.9 58.6 all-gather.20
  407.2 63.4 reduce-scatter.7
  474.0 63.7 reduce-scatter.9
  541.1 63.8 reduce-scatter.11
  608.4 63.8 reduce-scatter.13
  675.7 73.5 reduce-scatter.15
  752.9 73.1 reduce-scatter.17
  829.6 73.3 reduce-scatter.19
  905.7 45.3 all-reduce.13
where the time goes:
time: 973 us; the launch traced here: 968 us
  waiting for transfers between devices  475 us (49%)
  local copies, waits for them, and re-layouts  262 us (27%)
  matrix products  101 us (10%)
  blocking collectives  80.6 us (8%)
  other arithmetic  32.6 us (3%)
  between operations  16.7 us (2%)
    unnamed x91, local copies, waits for them, and re-layouts  90.8 us
    reduce_scatter x1, waiting for transfers between devices, shards(): lax.psum_scatter(grad_w_gate.astype(jnp.bfloat16), 'shard', scatter_dimen...  77.1 us
    reduce_scatter x1, waiting for transfers between devices, shards(): lax.psum_scatter(grad_w_down.astype(jnp.bfloat16), 'shard', scatter_dimen...  76.8 us
    reduce_scatter x1, waiting for transfers between devices, shards(): lax.psum_scatter(grad_w_up.astype(jnp.bfloat16), 'shard', scatter_dimensi...  76.8 us
    reshape x1, local copies, waits for them, and re-layouts, diagonal_sums(): placed.reshape(heads, block_rows * width)  69.5 us
    unnamed x2, blocking collectives  58.1 us
    all_gather x1, waiting for transfers between devices, shards(): lax.all_gather(w_gate, 'shard', axis=0, tiled=True)  55.6 us
    all_gather x1, waiting for transfers between devices, shards(): lax.all_gather(w_down, 'shard', axis=0, tiled=True)  55.2 us
  transfers between devices with their start and end apart: 15, of which 8 were waited for; matrix products, arithmetic and copies ran while one was open for 34% of the time, Pallas kernels for 0%

commit v1 on v0

--- a/solution.py
+++ b/solution.py
@@ -178,7 +178,9 @@
         lax.all_gather(w_output, "shard", axis=0, tiled=True),
         lax.all_gather(w_gate, "shard", axis=0, tiled=True),
         lax.all_gather(w_up, "shard", axis=0, tiled=True),
-        lax.all_gather(w_down, "shard", axis=0, tiled=True),
+        jnp.concatenate(
+            lax.all_to_all(jnp.stack([w_down] * lax.axis_size("shard")), "shard", 0, 0), axis=0
+        ),
         lax.all_gather(norm_attn, "shard", axis=0, tiled=True),
         lax.all_gather(norm_ffn, "shard", axis=0, tiled=True),
         lax.all_gather(rel_bias, "shard", axis=0, tiled=True),

time: 973 us -> 1000 us (1.028)
  waiting for transfers between devices: 475 us -> 494 us
    reduce_scatter x1, waiting for transfers between devices: 32.4 us -> 53 us  [shards(): lax.psum_scatter(grad_w_output.astype(jnp.bfloat16), 'shard', scatter_dim...]
    unnamed x91 -> x89, local copies, waits for them, and re-layouts: 90.8 us -> 91.8 us
  transfers between devices with their start and end apart: 15 -> 16, of which waited for: 8 -> 8; matrix products, arithmetic and copies ran while one was open for 34% -> 34% of each run, Pallas kernels for 0% -> 0%
where the time goes in v1:
time: 1000 us; the launch traced here: 998 us
  waiting for transfers between devices  494 us (49%)
  local copies, waits for them, and re-layouts  265 us (26%)
  matrix products  102 us (10%)
  blocking collectives  82.7 us (8%)
  other arithmetic  32.5 us (3%)
  between operations  16.7 us (2%)
    unnamed x89, local copies, waits for them, and re-layouts  91.8 us
    reduce_scatter x1, waiting for transfers between devices, shards(): lax.psum_scatter(grad_w_down.astype(jnp.bfloat16), 'shard', scatter_dimen...  77 us
    reduce_scatter x1, waiting for transfers between devices, shards(): lax.psum_scatter(grad_w_up.astype(jnp.bfloat16), 'shard', scatter_dimensi...  76.9 us
    reduce_scatter x1, waiting for transfers between devices, shards(): lax.psum_scatter(grad_w_gate.astype(jnp.bfloat16), 'shard', scatter_dimen...  76.8 us
    reshape x1, local copies, waits for them, and re-layouts, diagonal_sums(): placed.reshape(heads, block_rows * width)  69.5 us
    unnamed x2, blocking collectives  60.6 us
    all_gather x1, waiting for transfers between devices, shards(): lax.all_gather(w_gate, 'shard', axis=0, tiled=True)  55.6 us
    all_gather x1, waiting for transfers between devices, shards(): lax.all_gather(w_down, 'shard', axis=0, tiled=True)  55.2 us
  transfers between devices with their start and end apart: 16, of which 8 were waited for; matrix products, arithmetic and copies ran while one was open for 34% of the time, Pallas kernels for 0%

profile of v1, /device:TPU:0, one launch (start us, length us, event | category | flops | bytes accessed | tf_op | source)
XLA Modules:
  0.0 998.2 jit_solution(10827685663267182535)
XLA Ops:
  15.6 23.2 %all-reduce.9 = (bf16[768]{0:T(1024)(128)(2,1)S(1)}, bf16[768]{0:T(1024)(128)(2,1)S(1)}) all-reduce(bf16[768]{0:T(1024)(128)(2,1)S(1)} %dynamic-update-slice, bf16[768]{0:T(1024)(128)(2,1)S(1)} %dynamic-update-slice.1), channel_id=1, replica_groups=mesh['rep'=4,'shard'=8] {'shard'}, use_global_device_ids=true, to_apply=%add.3 | all-reduce | flops 1536 | bytes 6144
  39.1 16.5 %all-gather = bf16[8,4,12]{2,1,0:T(4,128)(2,1)S(1)} all-gather(bf16[1,4,12]{2,1,0:T(4,128)(2,1)S(1)} %bitcast.98), channel_id=1, replica_groups=mesh['rep'=4,'shard'=8] {'shard'}, dimensions={0}, use_global_device_ids=true | all-gather | bytes 864 | tf_op jit(solution)/shard_map/all_gather | solution.py:186
  55.9 6.1 broadcast_in_dim.120
  62.0 5.8 pad.17
  67.9 29.2 %copy.64 = bf16[2,8,512,1024]{3,1,2,0:T(8,128)(2,1)S(1)} copy(bf16[2,8,512,1024]{3,2,1,0:T(8,128)(2,1)S(1)} %bitcast.79) | data formatting | bytes 33554432
  97.1 6.6 slice.15
  103.7 36.8 %reshape.152 = bf16[12,512,1023]{2,1,0:T(8,128)(2,1)} reshape(bf16[12,523776]{1,0:T(8,128)(2,1)} %slice.15) | data formatting | bytes 25141248 | tf_op jit(solution)/shard_map/while/body/eval_jaxpr/reshape | solution.py:52
  140.4 9.7 dynamic_slice.35
  150.2 8.7 copy.62
  159.2 2.1 convolution_convert_fusion.10
  161.3 2.1 convolution_convert_fusion.9
  164.0 3.3 convolution_convert_fusion.8
  168.7 5.3 fusion.43
  175.9 2.7 copy-done
  178.5 2.9 fusion.28
  181.5 2.5 multiply_reduce_fusion.3
  185.3 55.6 %all-gather.17.cloned.1.call-done = bf16[768,2048]{1,0:T(8,128)(2,1)} async-done(((bf16[96,2048]{1,0:T(8,128)(2,1)}), bf16[768,2048]{1,0:T(8,128)(2,1)}) %all-gather.17.cloned.1.call-update) | async-done | bytes 3145744 | tf_op jit(solution)/shard_map/all_gather | solution.py:179
  241.0 5.6 fusion.44
  246.6 55.1 %all-gather.19.cloned.1.call-done = bf16[768,2048]{1,0:T(8,128)(2,1)} async-done(((bf16[96,2048]{1,0:T(8,128)(2,1)}), bf16[768,2048]{1,0:T(8,128)(2,1)}) %all-gather.19.cloned.1.call-update) | async-done | bytes 3145744 | tf_op jit(solution)/shard_map/all_gather | solution.py:180
  301.7 5.7 fusion.45
  307.4 55.2 %all-gather.21.cloned.1.call-done = bf16[2048,768]{1,0:T(8,128)(2,1)} async-done(((bf16[256,768]{1,0:T(8,128)(2,1)}), bf16[2048,768]{1,0:T(8,128)(2,1)}) %all-gather.21.cloned.1.call-update) | async-done | bytes 3145744 | tf_op jit(solution)/shard_map/all_gather | solution.py:198
  362.6 8.6 multiply_convert_fusion.1
  381.7 10.6 %multiply_reduce_fusion = (f32[12,512]{1,0:T(8,128)S(1)}, f32[12,512,512]{1,2,0:T(8,128)}) fusion(f32[12,512,512]{1,2,0:T(8,128)} %copy-done, f32[12,512]{1,0:T(8,128)S(1)} %log_add_fusion, bf16[512,12,64]{0,2,1:T(8,128)(2,1)S(1)} %bitcast.83, bf16[512,12,64]{0,2,1:T(8,128)(2,1)} %bitcast.88), kind=kOutput, calls=%fused_computation.2 | convolution fusion | flops 412084224 | bytes 26787840 | tf_op jit(solution)/shard_map/while/body/eval_jaxpr/qhd,khd->hqk/dot_general | solution.py:260
  394.5 7.0 multiply_convert_fusion
  407.1 5.1 multiply_convert_fusion.3
  415.1 6.6 fusion.25
  426.7 5.4 convolution_convert_fusion.2
  433.2 5.1 convolution_convert_fusion.1
  439.4 5.1 convolution_convert_fusion
  447.3 4.4 all-to-all-start
  453.1 8.7 copy.63
  461.8 9.4 dynamic_update_slice.15.clone
  471.2 69.5 %reshape.155 = bf16[12,785920]{1,0:T(8,128)(2,1)} reshape(bf16[12,512,1535]{2,1,0:T(8,128)(2,1)} %dynamic_update_slice.15.clone) | data formatting | bytes 37724160 | tf_op jit(solution)/shard_map/while/body/eval_jaxpr/reshape | solution.py:65
  540.6 13.1 %pad.16 = bf16[12,786432]{1,0:T(8,128)(2,1)S(1)} pad(bf16[12,785920]{1,0:T(8,128)(2,1)} %reshape.155, bf16[]{:T(256)} %constant.111.clone.1), padding=0_0x0_512 | pad | bytes 37736448 | tf_op jit(solution)/shard_map/while/body/eval_jaxpr/jit(_pad)/pad | solution.py:65
  553.7 19.4 %copy.65 = bf16[2,8,512,1536]{3,2,1,0:T(8,128)(2,1)} copy(bf16[2,8,512,1536]{3,1,2,0:T(8,128)(2,1)S(1)} %bitcast.77) | data formatting | bytes 50331648
  573.2 16.6 %slice.17 = bf16[12,512,1536]{2,1,0:T(8,128)(2,1)} slice(bf16[16,512,1536]{2,1,0:T(8,128)(2,1)} %bitcast.78), slice={[0:12], [0:512], [0:1536]} | slice | bytes 37748736 | tf_op jit(solution)/shard_map/while/body/eval_jaxpr/reshape | solution.py:66
  589.8 7.8 convert_reduce_fusion
  598.2 2.1 fusion.47
  601.9 2.4 fusion.23
  604.3 37.5 %all-reduce.8 = (bf16[768]{0:T(1024)(128)(2,1)S(1)}, bf16[768]{0:T(1024)(128)(2,1)S(1)}, bf16[32,12]{1,0:T(8,128)(2,1)S(1)}) all-reduce(bf16[768]{0:T(1024)(128)(2,1)S(1)} %get-tuple-element.78, bf16[768]{0:T(1024)(128)(2,1)S(1)} %get-tuple-element.76, ...), channel_id=9, replica_groups=mesh['rep'=4,'shard'=8] {'shard'}, use_global_device_ids=true, to_apply=%region_22.23.clone | all-reduce | flops 1920 | bytes 7680
  641.9 5.6 all-reduce.10
  649.2 53.0 %reduce-scatter.14.cloned.1.call-done = bf16[96,768]{1,0:T(8,128)(2,1)} async-done(((bf16[768,768]{1,0:T(8,128)(2,1)}), bf16[96,768]{1,0:T(8,128)(2,1)}) %reduce-scatter.14.cloned.1.call-update) | async-done | bytes 147472 | tf_op jit(solution)/shard_map/reduce_scatter | solution.py:331
  702.2 76.8 %reduce-scatter.16.cloned.1.call-done = bf16[96,2048]{1,0:T(8,128)(2,1)} async-done(((bf16[768,2048]{1,0:T(8,128)(2,1)}), bf16[96,2048]{1,0:T(8,128)(2,1)}) %reduce-scatter.16.cloned.1.call-update) | async-done | bytes 393232 | tf_op jit(solution)/shard_map/reduce_scatter | solution.py:334
  779.0 76.9 %reduce-scatter.18.cloned.1.call-done = bf16[96,2048]{1,0:T(8,128)(2,1)} async-done(((bf16[768,2048]{1,0:T(8,128)(2,1)}), bf16[96,2048]{1,0:T(8,128)(2,1)}) %reduce-scatter.18.cloned.1.call-update) | async-done | bytes 393232 | tf_op jit(solution)/shard_map/reduce_scatter | solution.py:337
  855.9 77.0 %reduce-scatter.20.cloned.1.call-done = bf16[256,768]{1,0:T(8,128)(2,1)} async-done(((bf16[2048,768]{1,0:T(8,128)(2,1)}), bf16[256,768]{1,0:T(8,128)(2,1)}) %reduce-scatter.20.cloned.1.call-update) | async-done | bytes 393232 | tf_op jit(solution)/shard_map/reduce_scatter | solution.py:340
  932.9 2.7 fusion.22
  935.6 5.7 add_convert_fusion
  941.3 39.6 %all-reduce.14.cloned.1.call-done = (bf16[96,768]{1,0:T(8,128)(2,1)}, bf16[96,768]{1,0:T(8,128)(2,1)}, bf16[96,768]{1,0:T(8,128)(2,1)}, bf16[96,768]{1,0:T(8,128...) async-done(((bf16[96,768]{1,0:T(8,128)(2,1)}, bf16[96,768]{1,0:T(8,128)(2,1)}, bf16[96,768]{1,0:T(8,128)(2,1)}, ...) | async-done | bytes 1769488 | tf_op jit(solution)/shard_map/psum | solution.py:354
  (161 shorter events, 59.1 us)
Async XLA Ops:
  7.2 31.6 %copy-start.2 = (bf16[512,768]{1,0:T(8,128)(2,1)S(1)}, bf16[512,768]{1,0:T(8,128)(2,1)}, u32[]{:S(2)}) copy-start(bf16[512,768]{1,0:T(8,128)(2,1)} %param.14) | copy-start | bytes 2359300
  7.2 31.9 %copy-start.26 = (bf16[4,12]{1,0:T(4,128)(2,1)S(1)}, bf16[4,12]{1,0:T(4,128)(2,1)}, u32[]{:S(2)}) copy-start(bf16[4,12]{1,0:T(4,128)(2,1)} %param.26) | copy-start | bytes 292
  7.2 48.3 %copy-start.31 = (s32[1023]{0:T(1024)S(1)}, s32[1023]{0:T(1024)}, u32[]{:S(2)}) copy-start(s32[1023]{0:T(1024)} %param.16) | copy-start | bytes 12280
  7.2 151.9 %all-gather.9.cloned.1.call-start = ((), (), s32[]{:S(2)}) async-start(), calls=%async_computation.8 | async-start | bytes 1327104 | tf_op jit(solution)/shard_map/all_gather | solution.py:177
  7.9 153.3 %all-gather.11.cloned.1.call-start = ((), (), s32[]{:S(2)}) async-start(), calls=%async_computation.9 | async-start | bytes 1327104 | tf_op jit(solution)/shard_map/all_gather | solution.py:175
  8.7 155.3 %all-gather.13.cloned.1.call-start = ((), (), s32[]{:S(2)}) async-start(), calls=%async_computation.10 | async-start | bytes 1327104 | tf_op jit(solution)/shard_map/all_gather | solution.py:176
  9.4 172.0 %all-gather.15.cloned.1.call-start = ((), (), s32[]{:S(2)}) async-start(), calls=%async_computation.11 | async-start | bytes 1327104 | tf_op jit(solution)/shard_map/all_gather | solution.py:178
  10.0 231.0 %all-gather.17.cloned.1.call-start = ((), (), s32[]{:S(2)}) async-start(), calls=%async_computation.12 | async-start | bytes 3538944 | tf_op jit(solution)/shard_map/all_gather | solution.py:179
  10.6 291.1 %all-gather.19.cloned.1.call-start = ((), (), s32[]{:S(2)}) async-start(), calls=%async_computation.13 | async-start | bytes 3538944 | tf_op jit(solution)/shard_map/all_gather | solution.py:180
  11.2 351.4 %all-gather.21.cloned.1.call-start = ((), (), s32[]{:S(2)}) async-start(), calls=%async_computation.14 | async-start | bytes 3538944 | tf_op jit(solution)/shard_map/all_gather | solution.py:198
  11.9 637.3 %reduce-scatter.8.cloned.1.call-start = ((), (), s32[]{:S(2)}) async-start(), calls=%async_computation.15 | async-start | bytes 1327104 | tf_op jit(solution)/shard_map/reduce_scatter | solution.py:322
  150.2 8.7 copy-start.25
  163.7 12.2 %copy-start.8 = (bf16[512,768]{0,1:T(8,128)(2,1)}, bf16[512,768]{0,1:T(8,128)(2,1)S(1)}, u32[]{:S(2)}) copy-start(bf16[512,768]{0,1:T(8,128)(2,1)S(1)} %copy.48) | copy-start | bytes 2359300
  164.0 4.7 copy-start.5
  174.0 4.5 copy-start
  181.4 2.5 copy-start.15
  184.0 1.2 copy-start.6
  185.3 116.4 %copy-start.17 = (bf16[512,768]{1,0:T(8,128)(2,1)}, bf16[512,768]{1,0:T(8,128)(2,1)S(1)}, u32[]{:S(2)}) copy-start(bf16[512,768]{1,0:T(8,128)(2,1)S(1)} %multiply_convert_fusion.5) | copy-start | bytes 2359300
  246.6 116.0 %copy-start.19 = (bf16[512,768]{1,0:T(8,128)(2,1)S(1)}, bf16[512,768]{1,0:T(8,128)(2,1)}, u32[]{:S(2)}) copy-start(bf16[512,768]{1,0:T(8,128)(2,1)} %param.27) | copy-start | bytes 2359300
  362.6 8.6 copy-start.27
  371.2 1.9 copy-start.34
  371.2 2.1 copy-start.33
  371.3 2.6 copy-start.7
  371.3 3.9 copy-start.28
  377.2 1.3 copy-start.30
  381.6 10.7 %slice-start = ((s8[12582912]{0:T(1024)(128)(4,1)}), s8[4194304]{0:T(1024)(128)(4,1)S(1)}, s32[]{:S(2)}) async-start(s8[12582912]{0:T(1024)(128)(4,1)} %bitcast.75), calls=%async_computation.23 | async-start | bytes 8388608
  381.6 11.6 %slice-start.1 = ((s8[12582912]{0:T(1024)(128)(4,1)}), s8[4194304]{0:T(1024)(128)(4,1)S(1)}, s32[]{:S(2)}) async-start(s8[12582912]{0:T(1024)(128)(4,1)} %bitcast.75), calls=%async_computation.24 | async-start | bytes 8388608
  381.6 12.8 %slice-start.2 = ((s8[12582912]{0:T(1024)(128)(4,1)}), s8[4194304]{0:T(1024)(128)(4,1)S(1)}, s32[]{:S(2)}) async-start(s8[12582912]{0:T(1024)(128)(4,1)} %bitcast.75), calls=%async_computation.25 | async-start | bytes 8388608
  401.5 2.6 copy-start.1
  401.5 3.5 copy-start.3
  407.0 6.0 copy-start.4
  407.0 242.2 %reduce-scatter.10.cloned.1.call-start = ((), (), s32[]{:S(2)}) async-start(), calls=%async_computation.16 | async-start | bytes 1327104 | tf_op jit(solution)/shard_map/reduce_scatter | solution.py:325
  415.1 234.1 %reduce-scatter.12.cloned.1.call-start = ((), (), s32[]{:S(2)}) async-start(), calls=%async_computation.17 | async-start | bytes 1327104 | tf_op jit(solution)/shard_map/reduce_scatter | solution.py:328
  422.7 2.1 copy-start.16
  424.7 277.5 %reduce-scatter.14.cloned.1.call-start = ((), (), s32[]{:S(2)}) async-start(), calls=%async_computation.18 | async-start | bytes 1327104 | tf_op jit(solution)/shard_map/reduce_scatter | solution.py:331
  426.6 352.4 %reduce-scatter.16.cloned.1.call-start = ((), (), s32[]{:S(2)}) async-start(), calls=%async_computation.19 | async-start | bytes 3538944 | tf_op jit(solution)/shard_map/reduce_scatter | solution.py:334
  432.0 423.8 %reduce-scatter.18.cloned.1.call-start = ((), (), s32[]{:S(2)}) async-start(), calls=%async_computation.20 | async-start | bytes 3538944 | tf_op jit(solution)/shard_map/reduce_scatter | solution.py:337
  438.3 494.6 %reduce-scatter.20.cloned.1.call-start = ((), (), s32[]{:S(2)}) async-start(), calls=%async_computation.21 | async-start | bytes 3538944 | tf_op jit(solution)/shard_map/reduce_scatter | solution.py:340
  447.3 488.3 %all-to-all-start = ((bf16[8,256,768]{2,1,0:T(8,128)(2,1)}), bf16[8,256,768]{2,1,0:T(8,128)(2,1)}, u32[]{:S(2)}, u32[]{:S(2)}) async-start(bf16[8,256,768]{2,1,0:T(8,128)(2,1)} %stack.2), calls=%async_computation | async-start | bytes 6291456 | tf_op jit(solution)/shard_map/all_to_all | solution.py:182
  451.8 529.1 %all-reduce.14.cloned.1.call-start = ((), (), s32[]{:S(2)}) async-start(), calls=%async_computation.22 | async-start | bytes 3538944 | tf_op jit(solution)/shard_map/psum | solution.py:354
  589.8 7.8 copy-start.32
  589.8 8.5 copy-start.12
  597.6 2.7 copy-start.22
  597.6 2.7 copy-start.29
  600.4 1.1 copy-start.10
  600.4 1.5 copy-start.14
  980.9 8.6 copy-start.24
  980.9 9.5 copy-start.23
  (6 other events, 5.9 us)
Sparse Core Ops, SparseCore 0:
  10.2 43.9 all-gather.8
  56.4 39.8 all-gather.10
  98.5 39.7 all-gather.12
  140.3 39.7 all-gather.14
  182.2 58.7 all-gather.16
  243.0 58.6 all-gather.18
  303.9 58.6 all-gather.20
  407.1 69.6 reduce-scatter.7
  480.2 87.6 reduce-scatter.9
  571.1 63.9 reduce-scatter.11
  638.5 63.6 reduce-scatter.13
  705.6 73.3 reduce-scatter.15
  782.6 73.2 reduce-scatter.17
  859.3 73.5 reduce-scatter.19
  935.6 45.3 all-reduce.13
